TPU v7x, 32 devices: a whole 2x2x4 slice. The times are simulated.
32 devices in a mesh: dom: 4 (over y, x), tp: 8 (over z, core).
Axes of the slice: x: 2, y: 2, z: 4, core: 2. Of those that a mesh axis runs over, the one named last changes fastest.
Arguments:
- latent: bfloat16 [1024, 16384], P('tp', 'dom'), may hold values from -6 to 6
- w_first: bfloat16 [1024, 1024], P(None, 'tp'), may hold values from -0.1875 to 0.1875
- w_second: bfloat16 [1024, 1024], P('tp'), may hold values from -0.1875 to 0.1875
- w_env: bfloat16 [1024, 256], P('tp'), may hold values from -0.1875 to 0.1875
- edge_vec: float32 [3, 16384], P(None, 'dom'), may hold values from -3 to 3, as said below
- centers: int32 [16384], P('dom'), may hold values from 0 to 127
- block_dest: int32 [128, 1], P('dom'), may hold values from 0 to 3; in each aligned block of 32 rows (0 to 31, 32 to 63, ...) at most 16 rows name the same one
- block_fill: int32 [128], P('dom'), may hold values from 64 to 128
- species: int32 [512], P('dom'), may hold values from 0 to 3
- species_gain: float32 [4, 256], P(None, 'tp'), may hold values from 0.1 to 1.9
Outputs:
- latent_new: bfloat16 [1024, 16384], P('tp', 'dom')
- env_out: float32 [9, 256, 512], P(None, 'tp', 'dom')
- invariants: float32 [3, 256, 16384], P(None, 'tp', 'dom')
Inputs may be any that keep to these rules, and one draw needn't show every extreme that they name: `block_dest`: in the 32 blocks of one domain no destination domain is named more than 16 times, a bound that some block reaches. `edge_vec`: every component has magnitude 0.5 to 3.
All inputs are finite; a program needn't handle non-finite values.
Results may differ from a plain program's by a relative error of at most 0.0077.
Values may be sent and summed in bfloat16 or wider, within the bound.
No kernel may reach another device: no remote copies, remote signals or barrier semaphores. Data moves between devices by JAX's collectives and lax.ppermute only.
A program may use at most 128 MiB of HBM per device.

v0:
```python
import functools
import math

import jax
import jax.numpy as jnp
from jax import lax
from jax.experimental import pallas as pl
from jax.experimental.pallas import tpu as pltpu
from jax.sharding import PartitionSpec as P


root_three = math.sqrt(3.0)
root_five = math.sqrt(5.0)
root_fifteen = math.sqrt(15.0)
cutoff_radius = 6.0
env_factor = 0.25
lanes = 128
cores = 2
bf16 = jnp.bfloat16
f32 = jnp.float32


mib = 1024 * 1024
in_vmem = pl.BlockSpec(memory_space=pltpu.VMEM)
in_smem = pl.BlockSpec(memory_space=pltpu.SMEM)


def harmonics(vectors):
    along_x = vectors[0]
    along_y = vectors[1]
    along_z = vectors[2]
    radius = jnp.sqrt(along_x * along_x + along_y * along_y + along_z * along_z)
    unit_x = along_x / radius
    unit_y = along_y / radius
    unit_z = along_z / radius
    ratio = radius / cutoff_radius
    envelope = (1.0 - ratio * ratio) ** 2
    parts = [
        jnp.ones_like(unit_x),
        root_three * unit_x,
        root_three * unit_y,
        root_three * unit_z,
        root_fifteen * unit_x * unit_y,
        root_fifteen * unit_y * unit_z,
        root_five / 2.0 * (3.0 * unit_z * unit_z - 1.0),
        root_fifteen * unit_x * unit_z,
        root_fifteen / 2.0 * (unit_x * unit_x - unit_y * unit_y),
    ]
    return [part * envelope for part in parts]


def contract_rows(left, right):
    return lax.dot_general(
        left, right, (((0,), (0,)), ((), ())), preferred_element_type=f32
    )


def swap_blocks(array, axis):
    return lax.all_to_all(array, axis, split_axis=0, concat_axis=0, tiled=True)


def flip_dom(array, mask):
    count = lax.axis_size("dom")
    return lax.ppermute(array, "dom", [(i, i ^ mask) for i in range(count)])


def shift_chips(array, step):
    count = lax.axis_size("tp")
    chips = count // cores
    pairs = [(t, (t // cores + step) % chips * cores + t % cores) for t in range(count)]
    return lax.ppermute(array, "tp", pairs)


def flip_tp(array, mask):
    count = lax.axis_size("tp")
    return lax.ppermute(array, "tp", [(t, t ^ mask) for t in range(count)])


def other_core(array):
    return flip_tp(array, 1)


def prepare_kernel(me_ref, first_ref, second_ref, env_ref, full_ref, own_ref):
    quarters = full_ref.shape[0]
    width = first_ref.shape[0] // quarters
    chan = env_ref.shape[1] // quarters
    for q in range(quarters):
        row = 0
        for start in range(q * width, (q + 1) * width, lanes):
            full_ref[q, row : row + lanes, :] = first_ref[start : start + lanes, :].T
            row += lanes
        full_ref[q, row : row + width, :] = second_ref[:, q * width : (q + 1) * width].T
        row += width
        full_ref[q, row : row + chan, :] = env_ref[:, q * chan : (q + 1) * chan].T
    own_ref[...] = full_ref[me_ref[0]]


def mlp_kernel(me_ref, x_ref, *refs, quarters, chips, chan, batches):
    per_group = 1 + len(batches) * quarters
    sources = [refs[g * per_group : (g + 1) * per_group] for g in range(cores)]
    shards, depth, _ = x_ref.shape
    outs = refs[cores * per_group :]
    new_refs, (out_ref, first, second, env, moved, hidden, fresh) = outs[:shards], outs[shards:]
    total = shards * depth
    width = total // quarters
    per_quarter = shards // quarters
    dom, chip, core = me_ref[0], me_ref[1], me_ref[2]
    for j in range(quarters):
        for i in range(per_quarter):
            start = j * width + i * depth
            moved[start : start + depth, :] = x_ref[(dom ^ j) * per_quarter + i]
    order = [(0, None, 0)]
    for batch, steps in enumerate(batches):
        order += [(k, batch, at) for at, k in enumerate(steps)]
    for k, batch, within in order:
        for g in range(cores):
            at = (k * cores + g) * depth
            for j in range(quarters):
                if batch is None:
                    block = sources[g][0].at[dom ^ j]
                else:
                    block = sources[g][1 + batch * quarters + j].at[within]
                for i in range(width // lanes):
                    place = j * width + i * lanes
                    first[at : at + depth, place : place + lanes] = block[
                        i * depth : (i + 1) * depth, :
                    ]
                row = width // lanes * depth
                place = pl.multiple_of((dom ^ j) * width, lanes)
                second[pl.ds(place, width), at : at + depth] = block[row : row + width, :]
                row += width
                place = pl.multiple_of((dom ^ j) * chan, chan)
                env[pl.ds(place, chan), at : at + depth] = block[row : row + chan, :]
    value = jnp.dot(first[...], moved[...], preferred_element_type=f32)
    hidden[...] = (value / (1.0 + jnp.exp(-value))).astype(bf16)
    update = jnp.dot(second[...], hidden[...], preferred_element_type=f32)
    for s in range(shards):
        rows = slice(s * depth, (s + 1) * depth)
        fresh[s] = (x_ref[s].astype(f32) + update[rows, :]).astype(bf16)
    for s, out in enumerate(new_refs):
        out[...] = fresh[(chip * cores + core) ^ s]
    for k in range(chips):
        for g in range(cores):
            at = (k * cores + g) * depth
            source = lax.rem(chip + chips - k, chips) * cores + (core if g == 0 else 1 - core)
            moved[at : at + depth, :] = fresh[source]
    rows = jnp.dot(env[...], moved[...], preferred_element_type=f32).astype(bf16)
    per = rows.shape[0] // shards
    for s in range(shards):
        out_ref[s] = rows[s * per : (s + 1) * per, :]


def split_kernel(x_ref, tie_ref, out_ref):
    edges = out_ref.shape[2]
    for s in range(out_ref.shape[0]):
        out_ref[s] = x_ref[:, s * edges : (s + 1) * edges]


def join_kernel(me_ref, *refs):
    pieces, out_ref = refs[:-1], refs[-1]
    edges = pieces[0].shape[1]
    for s, piece in enumerate(pieces):
        at = pl.multiple_of((me_ref[0] ^ s) * edges, lanes)
        out_ref[:, pl.ds(at, edges)] = piece[...]


def spread_mlp(latent, w_first, w_second, w_env):
    domains = lax.axis_size("dom")
    shards = lax.axis_size("tp")
    chips = shards // cores
    total = w_first.shape[0]
    depth = w_first.shape[1]
    channels = w_env.shape[1]
    width = total // domains
    chan = channels // domains
    rows = 2 * width + chan
    edges = latent.shape[1] // shards
    dom = lax.axis_index("dom").astype(jnp.int32)
    place = lax.axis_index("tp").astype(jnp.int32)
    full, own = pl.pallas_call(
        prepare_kernel,
        out_shape=(
            jax.ShapeDtypeStruct((domains, rows, depth), bf16),
            jax.ShapeDtypeStruct((rows, depth), bf16),
        ),
        in_specs=[in_smem, in_vmem, in_vmem, in_vmem],
        out_specs=(in_vmem, in_vmem),
        compiler_params=pltpu.CompilerParams(vmem_limit_bytes=8 * mib),
        name="prepare",
    )(dom[None], w_first, w_second, w_env)
    pieces = pl.pallas_call(
        split_kernel,
        out_shape=jax.ShapeDtypeStruct((shards, depth, edges), bf16),
        in_specs=[in_vmem, pl.BlockSpec(memory_space=pl.ANY)],
        out_specs=in_vmem,
        compiler_params=pltpu.CompilerParams(vmem_limit_bytes=8 * mib),
        name="split",
    )(latent, own)
    shifted = {k: shift_chips(own, k) for k in range(1, chips)}
    edge_rows = swap_blocks(pieces, "tp")
    near = [k for k in (1, chips - 1)]
    batches = [near, [k for k in range(2, chips - 1)]]
    mine = [full]
    for steps in batches:
        arrived = jnp.stack([shifted[k] for k in steps])
        mine += [arrived] + [flip_dom(arrived, j) for j in range(1, domains)]
    others = [other_core(array) for array in mine]
    me = jnp.stack([dom, place // cores, place % cores])
    *new_rows, weight_rows = pl.pallas_call(
        functools.partial(mlp_kernel, quarters=domains, chips=chips, chan=chan, batches=batches),
        out_shape=[jax.ShapeDtypeStruct((depth, edges), bf16)] * shards
        + [jax.ShapeDtypeStruct((shards, channels // shards, edges), bf16)],
        in_specs=[in_smem] + [in_vmem] * (1 + 2 * len(mine)),
        out_specs=[in_vmem] * (shards + 1),
        scratch_shapes=[
            pltpu.VMEM((total, total), bf16),
            pltpu.VMEM((total, total), bf16),
            pltpu.VMEM((channels, total), bf16),
            pltpu.VMEM((total, edges), bf16),
            pltpu.VMEM((total, edges), bf16),
            pltpu.VMEM((shards, depth, edges), bf16),
        ],
        compiler_params=pltpu.CompilerParams(vmem_limit_bytes=28 * mib),
        name="mlp",
    )(me, edge_rows, *mine, *others)
    weights = swap_blocks(weight_rows, "tp")
    back = [new_rows[0]] + [flip_tp(new_rows[s], s) for s in range(1, shards)]
    latent_new = pl.pallas_call(
        join_kernel,
        out_shape=jax.ShapeDtypeStruct(latent.shape, bf16),
        in_specs=[in_smem] + [in_vmem] * shards,
        out_specs=in_vmem,
        compiler_params=pltpu.CompilerParams(vmem_limit_bytes=8 * mib),
        name="join",
    )(place[None], *back)
    return latent_new, weights


def gathered_mlp(latent, w_first, w_second, w_env):
    edge_rows = lax.all_to_all(latent, "tp", split_axis=1, concat_axis=0, tiled=True)
    full_first = lax.all_gather(w_first, "tp", axis=1, tiled=True)
    full_second = lax.all_gather(w_second, "tp", axis=0, tiled=True)
    full_env = lax.all_gather(w_env, "tp", axis=0, tiled=True)
    hidden = jax.nn.silu(contract_rows(full_first, edge_rows)).astype(bf16)
    update = contract_rows(full_second, hidden)
    new_rows = (edge_rows.astype(f32) + update).astype(bf16)
    weight_rows = contract_rows(full_env, new_rows).astype(bf16)
    shards = lax.axis_size("tp")
    weights = swap_blocks(weight_rows.reshape(shards, -1, weight_rows.shape[1]), "tp")
    new_rows, weights = lax.optimization_barrier((new_rows, weights))
    return lax.all_to_all(new_rows, "tp", split_axis=0, concat_axis=1, tiled=True), weights


def geometry_kernel(vec_ref, fill_ref, out_ref):
    vectors = [vec_ref[i] for i in range(3)]
    ids = lax.broadcasted_iota(jnp.int32, vectors[0].shape, 1)
    alive = (ids < fill_ref[...]).astype(f32)
    for m, part in enumerate(harmonics(vectors)):
        out_ref[m] = part * alive


def select_atoms(centers_ref, block, atoms):
    ids = lax.broadcasted_iota(jnp.int32, (atoms, lanes), 0)
    return (ids == centers_ref[pl.ds(block, 1), :]).astype(f32).astype(bf16)


def sums_kernel(dest_ref, me_ref, w_ref, h_ref, centers_ref, *refs):
    outs, total = refs[:-1], refs[-1]
    shards, _, edges = w_ref.shape
    atoms = total.shape[2]
    per = edges // lanes
    total[...] = jnp.zeros_like(total)

    def step(s, carry):
        for i in range(per):
            block = s * per + i
            weight = w_ref[s, :, i * lanes : (i + 1) * lanes].astype(f32)
            parts = [
                (h_ref[m, pl.ds(block, 1), :] * weight).astype(bf16)
                for m in range(h_ref.shape[0])
            ]
            contrib = jnp.concatenate(parts, axis=0)
            chosen = select_atoms(centers_ref, block, atoms)
            slot = dest_ref[block] ^ me_ref[0]
            total[slot] += lax.dot_general(
                contrib, chosen, (((1,), (1,)), ((), ())), preferred_element_type=f32
            )
        return carry

    lax.fori_loop(0, shards, step, 0)
    for j, out in enumerate(outs):
        out[...] = total[j].astype(out.dtype)


def invariants_kernel(dest_ref, me_ref, w_ref, h_ref, centers_ref, *refs):
    domains = len(refs) - 2
    out_ref, env = refs[domains:]
    shards, chan, edges = w_ref.shape
    atoms = env.shape[2]
    per = edges // lanes
    for j in range(domains):
        env[j] = refs[j][...]

    def step(s, carry):
        for i in range(per):
            block = s * per + i
            weight = w_ref[s, :, i * lanes : (i + 1) * lanes].astype(f32)
            chosen = select_atoms(centers_ref, block, atoms)
            slot = dest_ref[block] ^ me_ref[0]
            found = jnp.dot(env[slot], chosen, preferred_element_type=f32)
            products = [
                found[m * chan : (m + 1) * chan, :] * h_ref[m, pl.ds(block, 1), :]
                for m in range(h_ref.shape[0])
            ]
            at = pl.multiple_of(block * lanes, lanes)
            out_ref[0, :, pl.ds(at, lanes)] = products[0] * weight
            out_ref[1, :, pl.ds(at, lanes)] = sum(products[2:4], products[1]) * weight
            out_ref[2, :, pl.ds(at, lanes)] = sum(products[5:9], products[4]) * weight
        return carry

    lax.fori_loop(0, shards, step, 0)


def on_device(
    latent,
    w_first,
    w_second,
    w_env,
    edge_vec,
    centers,
    block_dest,
    block_fill,
    species,
    species_gain,
):
    domains = lax.axis_size("dom")
    shards = lax.axis_size("tp")
    nblocks = block_fill.shape[0]
    atoms = species.shape[0]
    chan = species_gain.shape[1]
    depth, edges = latent.shape
    me = lax.axis_index("dom").astype(jnp.int32)[None]
    spread = (
        depth == lanes
        and w_first.shape[0] % (domains * lanes) == 0
        and w_env.shape[1] % (domains * 16) == 0
        and shards % cores == 0
    )
    mlp = spread_mlp if spread else gathered_mlp
    latent_new, weights = mlp(latent, w_first, w_second, w_env)

    harmonic = pl.pallas_call(
        geometry_kernel,
        out_shape=jax.ShapeDtypeStruct((9, nblocks, lanes), f32),
        in_specs=[in_vmem, in_vmem],
        out_specs=in_vmem,
        compiler_params=pltpu.CompilerParams(vmem_limit_bytes=4 * mib),
        name="geometry",
    )(edge_vec.reshape(3, nblocks, lanes), block_fill[:, None])
    center_blocks = centers.reshape(nblocks, lanes)
    target = block_dest[:, 0]
    species_ids = jnp.arange(species_gain.shape[0], dtype=jnp.int32)
    gain_sel = jnp.sum(
        jnp.where(
            species[None, None, :] == species_ids[:, None, None], species_gain[:, :, None], 0.0
        ),
        axis=0,
    )

    rows = 9 * chan
    sums = pl.pallas_call(
        sums_kernel,
        out_shape=[jax.ShapeDtypeStruct((rows, atoms), f32)]
        + [jax.ShapeDtypeStruct((rows, atoms), bf16)] * (domains - 1),
        in_specs=[in_smem, in_smem] + [in_vmem] * 3,
        out_specs=[in_vmem] * domains,
        scratch_shapes=[pltpu.VMEM((domains, rows, atoms), f32)],
        compiler_params=pltpu.CompilerParams(vmem_limit_bytes=8 * mib),
        name="sums",
    )(target, me, weights, harmonic, center_blocks)
    env_raw = sums[0]
    for j in range(1, domains):
        env_raw = env_raw + flip_dom(sums[j], j).astype(f32)
    env_out = env_raw.reshape(9, chan, atoms) * gain_sel[None, :, :] * env_factor
    env_half = env_out.astype(bf16).reshape(rows, atoms)
    looked = [env_half] + [flip_dom(env_half, j) for j in range(1, domains)]
    invariants = pl.pallas_call(
        invariants_kernel,
        out_shape=jax.ShapeDtypeStruct((3, chan, edges), f32),
        in_specs=[in_smem, in_smem] + [in_vmem] * (3 + domains),
        out_specs=in_vmem,
        scratch_shapes=[pltpu.VMEM((domains, rows, atoms), bf16)],
        compiler_params=pltpu.CompilerParams(vmem_limit_bytes=10 * mib),
        name="invariants",
    )(target, me, weights, harmonic, center_blocks, *looked)
    return (latent_new, env_out, invariants)


def solution(mesh):
    in_specs = (
        P("tp", "dom"),
        P(None, "tp"),
        P("tp", None),
        P("tp", None),
        P(None, "dom"),
        P("dom"),
        P("dom", None),
        P("dom"),
        P("dom"),
        P(None, "tp"),
    )
    out_specs = (P("tp", "dom"), P(None, "tp", "dom"), P(None, "tp", "dom"))

    return jax.shard_map(on_device, mesh=mesh, in_specs=in_specs, out_specs=out_specs, check_vma=False)
```

profile of v0, /device:TPU:0, one launch (start us, length us, event | category | flops | bytes accessed | tf_op | source)
XLA Modules:
  0.0 139.2 jit_solution(6790430328338824563)
XLA Ops:
  6.0 6.4 %all-to-all-start = ((bf16[8,128,512]{2,1,0:T(8,128)(2,1)}), bf16[8,128,512]{2,1,0:T(8,128)(2,1)S(1)}, u32[]{:S(2)}, u32[]{:S(2)}) async-start(bf16[8,128,512]{2,1,0:T(8,128)(2,1)} %split.1), calls=%async_computation | async-start | bytes 2097152 | tf_op jit(solution)/shard_map/all_to_all | solution.py:59
  12.3 2.9 %collective-permute-start.5 = (bf16[576,128]{1,0:T(8,128)(2,1)S(1)}, bf16[576,128]{1,0:T(8,128)(2,1)S(1)}, u32[]{:S(2)}, u32[]{:S(2)}) collective-permute-start(bf16[576,128]{1,0:T(8,128)(2,1)S(1)} %get-tuple-element.18.tie_ref), channel_id=1, source_target_pairs={{0,4},{1,5},{2,6},{3,7},{4,0},{5,1},{6,2},{7,3},{8,12},{9,13},{10,... | collective-permute-start | bytes 442376 | tf_op jit(solution)/shard_map/ppermute | solution.py:71
  15.3 1.5 %collective-permute-start = (bf16[576,128]{1,0:T(8,128)(2,1)S(1)}, bf16[576,128]{1,0:T(8,128)(2,1)S(1)}, u32[]{:S(2)}, u32[]{:S(2)}) collective-permute-start(bf16[576,128]{1,0:T(8,128)(2,1)S(1)} %get-tuple-element.18.tie_ref), channel_id=1, source_target_pairs={{0,2},{1,3},{2,4},{3,5},{4,6},{5,7},{6,0},{7,1},{8,10},{9,11},{10,... | collective-permute-start | bytes 442376 | tf_op jit(solution)/shard_map/ppermute | solution.py:71
  16.7 2.4 %collective-permute-start.1 = (bf16[576,128]{1,0:T(8,128)(2,1)S(1)}, bf16[576,128]{1,0:T(8,128)(2,1)S(1)}, u32[]{:S(2)}, u32[]{:S(2)}) collective-permute-start(bf16[576,128]{1,0:T(8,128)(2,1)S(1)} %get-tuple-element.18.tie_ref), channel_id=1, source_target_pairs={{0,6},{1,7},{2,0},{3,1},{4,2},{5,3},{6,4},{7,5},{8,14},{9,15},{10,... | collective-permute-start | bytes 442376 | tf_op jit(solution)/shard_map/ppermute | solution.py:71
  19.1 29.9 %collective-permute-done.5 = bf16[576,128]{1,0:T(8,128)(2,1)S(1)} collective-permute-done((bf16[576,128]{1,0:T(8,128)(2,1)S(1)}, bf16[576,128]{1,0:T(8,128)(2,1)S(1)}, u32[]{:S(2)}, u32[]{:S(2)}) %collective-permute-start.5) | collective-permute-done | bytes 147488 | tf_op jit(solution)/shard_map/ppermute | solution.py:71
  49.0 1.5 %collective-permute-start.6 = (bf16[1,576,128]{2,1,0:T(8,128)(2,1)S(1)}, bf16[1,576,128]{2,1,0:T(8,128)(2,1)S(1)}, u32[]{:S(2)}, u32[]{:S(2)}) collective-permute-start(bf16[1,576,128]{2,1,0:T(8,128)(2,1)S(1)} %bitcast.22), channel_id=1, source_target_pairs={{0,8},{8,0},{16,24},{24,16},{1,9},{9,1},{17,25},{25,17},{2,10},{10... | collective-permute-start | bytes 442376 | tf_op jit(solution)/shard_map/ppermute | solution.py:64
  50.4 1.5 %collective-permute-start.7 = (bf16[1,576,128]{2,1,0:T(8,128)(2,1)S(1)}, bf16[1,576,128]{2,1,0:T(8,128)(2,1)S(1)}, u32[]{:S(2)}, u32[]{:S(2)}) collective-permute-start(bf16[1,576,128]{2,1,0:T(8,128)(2,1)S(1)} %bitcast.23), channel_id=1, source_target_pairs={{0,16},{8,24},{16,0},{24,8},{1,17},{9,25},{17,1},{25,9},{2,18},{10... | collective-permute-start | bytes 442376 | tf_op jit(solution)/shard_map/ppermute | solution.py:64
  52.5 1.6 %collective-permute-start.2 = (bf16[2,576,128]{2,1,0:T(8,128)(2,1)S(1)}, bf16[2,576,128]{2,1,0:T(8,128)(2,1)S(1)}, u32[]{:S(2)}, u32[]{:S(2)}) collective-permute-start(bf16[2,576,128]{2,1,0:T(8,128)(2,1)S(1)} %pad_maximum_fusion.refs_1_), channel_id=1, source_target_pairs={{0,8},{8,0},{16,24},{24,16},{1,9},{9,1},{17,25},{25,17},{2,10},{10... | collective-permute-start | bytes 884744 | tf_op jit(solution)/shard_map/ppermute | solution.py:64
  55.3 2.5 %collective-permute-done.7.refs_7_ = bf16[1,576,128]{2,1,0:T(8,128)(2,1)S(1)} collective-permute-done((bf16[1,576,128]{2,1,0:T(8,128)(2,1)S(1)}, bf16[1,576,128]{2,1,0:T(8,128)(2,1)S(1)}, u32[]{:S(2)}, u32[]{:S(2)}) %collective-permute-start.7) | collective-permute-done | bytes 147488 | tf_op jit(solution)/shard_map/ppermute | solution.py:64
  57.8 1.5 %collective-permute-start.3 = (bf16[2,576,128]{2,1,0:T(8,128)(2,1)S(1)}, bf16[2,576,128]{2,1,0:T(8,128)(2,1)S(1)}, u32[]{:S(2)}, u32[]{:S(2)}) collective-permute-start(bf16[2,576,128]{2,1,0:T(8,128)(2,1)S(1)} %pad_maximum_fusion.refs_1_), channel_id=1, source_target_pairs={{0,16},{8,24},{16,0},{24,8},{1,17},{9,25},{17,1},{25,9},{2,18},{10... | collective-permute-start | bytes 884744 | tf_op jit(solution)/shard_map/ppermute | solution.py:64
  61.2 3.8 %collective-permute-done.2.refs_2_ = bf16[2,576,128]{2,1,0:T(8,128)(2,1)S(1)} collective-permute-done((bf16[2,576,128]{2,1,0:T(8,128)(2,1)S(1)}, bf16[2,576,128]{2,1,0:T(8,128)(2,1)S(1)}, u32[]{:S(2)}, u32[]{:S(2)}) %collective-permute-start.2) | collective-permute-done | bytes 294944 | tf_op jit(solution)/shard_map/ppermute | solution.py:64
  65.6 6.0 %collective-permute-done.3.refs_3_ = bf16[2,576,128]{2,1,0:T(8,128)(2,1)S(1)} collective-permute-done((bf16[2,576,128]{2,1,0:T(8,128)(2,1)S(1)}, bf16[2,576,128]{2,1,0:T(8,128)(2,1)S(1)}, u32[]{:S(2)}, u32[]{:S(2)}) %collective-permute-start.3) | collective-permute-done | bytes 294944 | tf_op jit(solution)/shard_map/ppermute | solution.py:64
  83.3 5.0 %mlp.1 = (bf16[128,512]{1,0:T(8,128)(2,1)S(1)}, bf16[128,512]{1,0:T(8,128)(2,1)S(1)}, bf16[128,512]{1,0:T(8,128)(2,1)S(1)}, bf16[128,512]{1,0:T(8,128)(2,1)S(1)}...) custom-call(s32[3]{0:T(128)S(1)} %copy-done.21, ...), custom_call_target="tpu_custom_call" | custom-call | tf_op jit(solution)/shard_map/mlp/pallas_call | solution.py:209
  94.2 3.4 %all-to-all-start.1 = ((bf16[8,32,512]{2,1,0:T(8,128)(2,1)}), bf16[8,32,512]{2,1,0:T(8,128)(2,1)S(1)}, u32[]{:S(2)}, u32[]{:S(2)}) async-start(bf16[8,32,512]{2,1,0:T(8,128)(2,1)} %copy-done.3), calls=%async_computation.1 | async-start | bytes 524288 | tf_op jit(solution)/shard_map/all_to_all | solution.py:59
  98.0 1.6 %collective-permute-start.19 = (bf16[128,512]{1,0:T(8,128)(2,1)}, bf16[128,512]{1,0:T(8,128)(2,1)S(1)}, u32[]{:S(2)}, u32[]{:S(2)}) collective-permute-start(bf16[128,512]{1,0:T(8,128)(2,1)} %copy-done.29), channel_id=1, source_target_pairs={{0,2},{1,3},{2,0},{3,1},{4,6},{5,7},{6,4},{7,5},{8,10},{9,11},{10,... | collective-permute-start | bytes 393224 | tf_op jit(solution)/shard_map/ppermute | solution.py:76
  99.7 2.6 %collective-permute-start.21 = (bf16[128,512]{1,0:T(8,128)(2,1)}, bf16[128,512]{1,0:T(8,128)(2,1)S(1)}, u32[]{:S(2)}, u32[]{:S(2)}) collective-permute-start(bf16[128,512]{1,0:T(8,128)(2,1)} %copy-done.27), channel_id=1, source_target_pairs={{0,4},{1,5},{2,6},{3,7},{4,0},{5,1},{6,2},{7,3},{8,12},{9,13},{10,... | collective-permute-start | bytes 393224 | tf_op jit(solution)/shard_map/ppermute | solution.py:76
  102.4 3.5 %collective-permute-start.23 = (bf16[128,512]{1,0:T(8,128)(2,1)}, bf16[128,512]{1,0:T(8,128)(2,1)S(1)}, u32[]{:S(2)}, u32[]{:S(2)}) collective-permute-start(bf16[128,512]{1,0:T(8,128)(2,1)} %copy-done.25), channel_id=1, source_target_pairs={{0,6},{1,7},{2,4},{3,5},{4,2},{5,3},{6,0},{7,1},{8,14},{9,15},{10,... | collective-permute-start | bytes 393224 | tf_op jit(solution)/shard_map/ppermute | solution.py:76
  105.9 7.6 %collective-permute-done.19.refs_2_ = bf16[128,512]{1,0:T(8,128)(2,1)S(1)} collective-permute-done((bf16[128,512]{1,0:T(8,128)(2,1)}, bf16[128,512]{1,0:T(8,128)(2,1)S(1)}, u32[]{:S(2)}, u32[]{:S(2)}) %collective-permute-start.19) | collective-permute-done | bytes 131104 | tf_op jit(solution)/shard_map/ppermute | solution.py:76
  117.7 2.7 %sums.1 = (f32[288,128]{1,0:T(8,128)S(1)}, bf16[288,128]{1,0:T(8,128)(2,1)S(1)}, bf16[288,128]{1,0:T(8,128)(2,1)S(1)}, bf16[288,128]{1,0:T(8,128)(2,1)S(1)}) custom-call(s32[32]{0:T(128)S(1)} %bitcast.29, s32[1]{0:T(128)} %bitcast.1.me_ref, bf16[8,32,512]{2,1,0:T(8,128)(2,1)S(1)} %all-to-all-done.1.w_ref, f32[9,32,128]{2,1,0:T(8,128)S(1)} %geometry.1.h_ref, ...), custom_call_target="tpu_custom_call" | custom-call | tf_op jit(solution)/shard_map/sums/pallas_call | solution.py:371
  120.4 1.3 collective-permute-start.25
  126.7 1.5 %collective-permute-done.27 = bf16[288,128]{1,0:T(8,128)(2,1)S(1)} collective-permute-done((bf16[288,128]{1,0:T(8,128)(2,1)S(1)}, bf16[288,128]{1,0:T(8,128)(2,1)S(1)}, u32[]{:S(2)}, u32[]{:S(2)}) %collective-permute-start.27) | collective-permute-done | bytes 73760 | tf_op jit(solution)/shard_map/ppermute | solution.py:64
  129.9 1.9 %collective-permute-start.30 = (bf16[288,128]{1,0:T(8,128)(2,1)S(1)}, bf16[288,128]{1,0:T(8,128)(2,1)S(1)}, u32[]{:S(2)}, u32[]{:S(2)}) collective-permute-start(bf16[288,128]{1,0:T(8,128)(2,1)S(1)} %get-tuple-element.33.refs_0_), channel_id=1, source_target_pairs={{0,24},{8,16},{16,8},{24,0},{1,25},{9,17},{17,9},{25,1},{2,26},{10... | collective-permute-start | bytes 221192 | tf_op jit(solution)/shard_map/ppermute | solution.py:64
  133.8 1.8 %collective-permute-done.30.refs_3_ = bf16[288,128]{1,0:T(8,128)(2,1)S(1)} collective-permute-done((bf16[288,128]{1,0:T(8,128)(2,1)S(1)}, bf16[288,128]{1,0:T(8,128)(2,1)S(1)}, u32[]{:S(2)}, u32[]{:S(2)}) %collective-permute-start.30) | collective-permute-done | bytes 73760 | tf_op jit(solution)/shard_map/ppermute | solution.py:64
  135.6 3.6 %invariants.1 = f32[3,32,4096]{2,1,0:T(8,128)} custom-call(s32[32]{0:T(128)S(1)} %bitcast.30, s32[1]{0:T(128)} %bitcast.1.me_ref, bf16[8,32,512]{2,1,0:T(8,128)(2,1)S(1)} %all-to-all-done.1.w_ref, f32[9,32,128]{2,1,0:T(8,128)S(1)} %geometry.1.h_ref, s32[32,128]{1,0:T(8,128)S(1)} %bitcast.28, bf16[288,128]{1,0:T(8,128)(2,1)S(1)} %get-tuple-element.33.refs_0_, ...), custom_call_target="tpu_custom_call" | custom-call | tf_op jit(solution)/shard_map/invariants/pallas_call | solution.py:387
  (119 shorter events, 40.5 us)
Async XLA Ops:
  6.0 71.1 %all-to-all-start = ((bf16[8,128,512]{2,1,0:T(8,128)(2,1)}), bf16[8,128,512]{2,1,0:T(8,128)(2,1)S(1)}, u32[]{:S(2)}, u32[]{:S(2)}) async-start(bf16[8,128,512]{2,1,0:T(8,128)(2,1)} %split.1), calls=%async_computation | async-start | bytes 2097152 | tf_op jit(solution)/shard_map/all_to_all | solution.py:59
  12.3 36.6 %collective-permute-start.5 = (bf16[576,128]{1,0:T(8,128)(2,1)S(1)}, bf16[576,128]{1,0:T(8,128)(2,1)S(1)}, u32[]{:S(2)}, u32[]{:S(2)}) collective-permute-start(bf16[576,128]{1,0:T(8,128)(2,1)S(1)} %get-tuple-element.18.tie_ref), channel_id=1, source_target_pairs={{0,4},{1,5},{2,6},{3,7},{4,0},{5,1},{6,2},{7,3},{8,12},{9,13},{10,... | collective-permute-start | bytes 442376 | tf_op jit(solution)/shard_map/ppermute | solution.py:71
  15.3 37.2 %collective-permute-start = (bf16[576,128]{1,0:T(8,128)(2,1)S(1)}, bf16[576,128]{1,0:T(8,128)(2,1)S(1)}, u32[]{:S(2)}, u32[]{:S(2)}) collective-permute-start(bf16[576,128]{1,0:T(8,128)(2,1)S(1)} %get-tuple-element.18.tie_ref), channel_id=1, source_target_pairs={{0,2},{1,3},{2,4},{3,5},{4,6},{5,7},{6,0},{7,1},{8,10},{9,11},{10,... | collective-permute-start | bytes 442376 | tf_op jit(solution)/shard_map/ppermute | solution.py:71
  16.7 35.7 %collective-permute-start.1 = (bf16[576,128]{1,0:T(8,128)(2,1)S(1)}, bf16[576,128]{1,0:T(8,128)(2,1)S(1)}, u32[]{:S(2)}, u32[]{:S(2)}) collective-permute-start(bf16[576,128]{1,0:T(8,128)(2,1)S(1)} %get-tuple-element.18.tie_ref), channel_id=1, source_target_pairs={{0,6},{1,7},{2,0},{3,1},{4,2},{5,3},{6,4},{7,5},{8,14},{9,15},{10,... | collective-permute-start | bytes 442376 | tf_op jit(solution)/shard_map/ppermute | solution.py:71
  49.0 6.3 %collective-permute-start.6 = (bf16[1,576,128]{2,1,0:T(8,128)(2,1)S(1)}, bf16[1,576,128]{2,1,0:T(8,128)(2,1)S(1)}, u32[]{:S(2)}, u32[]{:S(2)}) collective-permute-start(bf16[1,576,128]{2,1,0:T(8,128)(2,1)S(1)} %bitcast.22), channel_id=1, source_target_pairs={{0,8},{8,0},{16,24},{24,16},{1,9},{9,1},{17,25},{25,17},{2,10},{10... | collective-permute-start | bytes 442376 | tf_op jit(solution)/shard_map/ppermute | solution.py:64
  50.4 7.3 %collective-permute-start.7 = (bf16[1,576,128]{2,1,0:T(8,128)(2,1)S(1)}, bf16[1,576,128]{2,1,0:T(8,128)(2,1)S(1)}, u32[]{:S(2)}, u32[]{:S(2)}) collective-permute-start(bf16[1,576,128]{2,1,0:T(8,128)(2,1)S(1)} %bitcast.23), channel_id=1, source_target_pairs={{0,16},{8,24},{16,0},{24,8},{1,17},{9,25},{17,1},{25,9},{2,18},{10... | collective-permute-start | bytes 442376 | tf_op jit(solution)/shard_map/ppermute | solution.py:64
  52.0 7.7 %collective-permute-start.8 = (bf16[1,576,128]{2,1,0:T(8,128)(2,1)S(1)}, bf16[1,576,128]{2,1,0:T(8,128)(2,1)}, u32[]{:S(2)}, u32[]{:S(2)}) collective-permute-start(bf16[1,576,128]{2,1,0:T(8,128)(2,1)S(1)} %bitcast.24), channel_id=1, source_target_pairs={{0,24},{8,16},{16,8},{24,0},{1,25},{9,17},{17,9},{25,1},{2,26},{10... | collective-permute-start | bytes 442376 | tf_op jit(solution)/shard_map/ppermute | solution.py:64
  52.4 8.1 %collective-permute-start.14 = (bf16[1,576,128]{2,1,0:T(8,128)(2,1)S(1)}, bf16[1,576,128]{2,1,0:T(8,128)(2,1)S(1)}, u32[]{:S(2)}, u32[]{:S(2)}) collective-permute-start(bf16[1,576,128]{2,1,0:T(8,128)(2,1)S(1)} %bitcast.25), channel_id=1, source_target_pairs={{0,1},{1,0},{2,3},{3,2},{4,5},{5,4},{6,7},{7,6},{8,9},{9,8},{10,11... | collective-permute-start | bytes 442376 | tf_op jit(solution)/shard_map/ppermute | solution.py:76
  52.5 12.5 %collective-permute-start.2 = (bf16[2,576,128]{2,1,0:T(8,128)(2,1)S(1)}, bf16[2,576,128]{2,1,0:T(8,128)(2,1)S(1)}, u32[]{:S(2)}, u32[]{:S(2)}) collective-permute-start(bf16[2,576,128]{2,1,0:T(8,128)(2,1)S(1)} %pad_maximum_fusion.refs_1_), channel_id=1, source_target_pairs={{0,8},{8,0},{16,24},{24,16},{1,9},{9,1},{17,25},{25,17},{2,10},{10... | collective-permute-start | bytes 884744 | tf_op jit(solution)/shard_map/ppermute | solution.py:64
  55.3 21.8 %collective-permute-start.9 = (bf16[4,576,128]{2,1,0:T(8,128)(2,1)S(1)}, bf16[4,576,128]{2,1,0:T(8,128)(2,1)S(1)}, u32[]{:S(2)}, u32[]{:S(2)}) collective-permute-start(bf16[4,576,128]{2,1,0:T(8,128)(2,1)S(1)} %get-tuple-element.19.refs_0_), channel_id=1, source_target_pairs={{0,1},{1,0},{2,3},{3,2},{4,5},{5,4},{6,7},{7,6},{8,9},{9,8},{10,11... | collective-permute-start | bytes 1769480 | tf_op jit(solution)/shard_map/ppermute | solution.py:76
  57.8 13.9 %collective-permute-start.3 = (bf16[2,576,128]{2,1,0:T(8,128)(2,1)S(1)}, bf16[2,576,128]{2,1,0:T(8,128)(2,1)S(1)}, u32[]{:S(2)}, u32[]{:S(2)}) collective-permute-start(bf16[2,576,128]{2,1,0:T(8,128)(2,1)S(1)} %pad_maximum_fusion.refs_1_), channel_id=1, source_target_pairs={{0,16},{8,24},{16,0},{24,8},{1,17},{9,25},{17,1},{25,9},{2,18},{10... | collective-permute-start | bytes 884744 | tf_op jit(solution)/shard_map/ppermute | solution.py:64
  59.7 12.6 %collective-permute-start.4 = (bf16[2,576,128]{2,1,0:T(8,128)(2,1)S(1)}, bf16[2,576,128]{2,1,0:T(8,128)(2,1)S(1)}, u32[]{:S(2)}, u32[]{:S(2)}) collective-permute-start(bf16[2,576,128]{2,1,0:T(8,128)(2,1)S(1)} %pad_maximum_fusion.refs_1_), channel_id=1, source_target_pairs={{0,24},{8,16},{16,8},{24,0},{1,25},{9,17},{17,9},{25,1},{2,26},{10... | collective-permute-start | bytes 884744 | tf_op jit(solution)/shard_map/ppermute | solution.py:64
  61.2 11.6 %collective-permute-start.10 = (bf16[2,576,128]{2,1,0:T(8,128)(2,1)S(1)}, bf16[2,576,128]{2,1,0:T(8,128)(2,1)S(1)}, u32[]{:S(2)}, u32[]{:S(2)}) collective-permute-start(bf16[2,576,128]{2,1,0:T(8,128)(2,1)S(1)} %pad_maximum_fusion.refs_1_), channel_id=1, source_target_pairs={{0,1},{1,0},{2,3},{3,2},{4,5},{5,4},{6,7},{7,6},{8,9},{9,8},{10,11... | collective-permute-start | bytes 884744 | tf_op jit(solution)/shard_map/ppermute | solution.py:76
  64.9 8.6 %collective-permute-start.15 = (bf16[1,576,128]{2,1,0:T(8,128)(2,1)S(1)}, bf16[1,576,128]{2,1,0:T(8,128)(2,1)S(1)}, u32[]{:S(2)}, u32[]{:S(2)}) collective-permute-start(bf16[1,576,128]{2,1,0:T(8,128)(2,1)S(1)} %collective-permute-done.6.refs_6_), channel_id=1, source_target_pairs={{0,1},{1,0},{2,3},{3,2},{4,5},{5,4},{6,7},{7,6},{8,9},{9,8},{10,11... | collective-permute-start | bytes 442376 | tf_op jit(solution)/shard_map/ppermute | solution.py:76
  94.2 22.1 %all-to-all-start.1 = ((bf16[8,32,512]{2,1,0:T(8,128)(2,1)}), bf16[8,32,512]{2,1,0:T(8,128)(2,1)S(1)}, u32[]{:S(2)}, u32[]{:S(2)}) async-start(bf16[8,32,512]{2,1,0:T(8,128)(2,1)} %copy-done.3), calls=%async_computation.1 | async-start | bytes 524288 | tf_op jit(solution)/shard_map/all_to_all | solution.py:59
  98.0 15.4 %collective-permute-start.19 = (bf16[128,512]{1,0:T(8,128)(2,1)}, bf16[128,512]{1,0:T(8,128)(2,1)S(1)}, u32[]{:S(2)}, u32[]{:S(2)}) collective-permute-start(bf16[128,512]{1,0:T(8,128)(2,1)} %copy-done.29), channel_id=1, source_target_pairs={{0,2},{1,3},{2,0},{3,1},{4,6},{5,7},{6,4},{7,5},{8,10},{9,11},{10,... | collective-permute-start | bytes 393224 | tf_op jit(solution)/shard_map/ppermute | solution.py:76
  99.7 20.7 %collective-permute-start.20 = (bf16[128,512]{1,0:T(8,128)(2,1)}, bf16[128,512]{1,0:T(8,128)(2,1)S(1)}, u32[]{:S(2)}, u32[]{:S(2)}) collective-permute-start(bf16[128,512]{1,0:T(8,128)(2,1)} %copy-done.28), channel_id=1, source_target_pairs={{0,3},{1,2},{2,1},{3,0},{4,7},{5,6},{6,5},{7,4},{8,11},{9,10},{10,... | collective-permute-start | bytes 393224 | tf_op jit(solution)/shard_map/ppermute | solution.py:76
  99.7 21.9 %collective-permute-start.21 = (bf16[128,512]{1,0:T(8,128)(2,1)}, bf16[128,512]{1,0:T(8,128)(2,1)S(1)}, u32[]{:S(2)}, u32[]{:S(2)}) collective-permute-start(bf16[128,512]{1,0:T(8,128)(2,1)} %copy-done.27), channel_id=1, source_target_pairs={{0,4},{1,5},{2,6},{3,7},{4,0},{5,1},{6,2},{7,3},{8,12},{9,13},{10,... | collective-permute-start | bytes 393224 | tf_op jit(solution)/shard_map/ppermute | solution.py:76
  102.3 20.5 %collective-permute-start.22 = (bf16[128,512]{1,0:T(8,128)(2,1)}, bf16[128,512]{1,0:T(8,128)(2,1)S(1)}, u32[]{:S(2)}, u32[]{:S(2)}) collective-permute-start(bf16[128,512]{1,0:T(8,128)(2,1)} %copy-done.26), channel_id=1, source_target_pairs={{0,5},{1,4},{2,7},{3,6},{4,1},{5,0},{6,3},{7,2},{8,13},{9,12},{10,... | collective-permute-start | bytes 393224 | tf_op jit(solution)/shard_map/ppermute | solution.py:76
  102.4 22.3 %collective-permute-start.23 = (bf16[128,512]{1,0:T(8,128)(2,1)}, bf16[128,512]{1,0:T(8,128)(2,1)S(1)}, u32[]{:S(2)}, u32[]{:S(2)}) collective-permute-start(bf16[128,512]{1,0:T(8,128)(2,1)} %copy-done.25), channel_id=1, source_target_pairs={{0,6},{1,7},{2,4},{3,5},{4,2},{5,3},{6,0},{7,1},{8,14},{9,15},{10,... | collective-permute-start | bytes 393224 | tf_op jit(solution)/shard_map/ppermute | solution.py:76
  113.5 11.3 %collective-permute-start.24 = (bf16[128,512]{1,0:T(8,128)(2,1)}, bf16[128,512]{1,0:T(8,128)(2,1)S(1)}, u32[]{:S(2)}, u32[]{:S(2)}) collective-permute-start(bf16[128,512]{1,0:T(8,128)(2,1)} %copy-done.24), channel_id=1, source_target_pairs={{0,7},{1,6},{2,5},{3,4},{4,3},{5,2},{6,1},{7,0},{8,15},{9,14},{10,... | collective-permute-start | bytes 393224 | tf_op jit(solution)/shard_map/ppermute | solution.py:76
  120.4 6.3 %collective-permute-start.25 = (bf16[288,128]{1,0:T(8,128)(2,1)S(1)}, bf16[288,128]{1,0:T(8,128)(2,1)S(1)}, u32[]{:S(2)}, u32[]{:S(2)}) collective-permute-start(bf16[288,128]{1,0:T(8,128)(2,1)S(1)} %get-tuple-element.30), channel_id=1, source_target_pairs={{0,8},{8,0},{16,24},{24,16},{1,9},{9,1},{17,25},{25,17},{2,10},{10... | collective-permute-start | bytes 221192 | tf_op jit(solution)/shard_map/ppermute | solution.py:64
  122.8 5.3 %collective-permute-start.27 = (bf16[288,128]{1,0:T(8,128)(2,1)S(1)}, bf16[288,128]{1,0:T(8,128)(2,1)S(1)}, u32[]{:S(2)}, u32[]{:S(2)}) collective-permute-start(bf16[288,128]{1,0:T(8,128)(2,1)S(1)} %get-tuple-element.32), channel_id=1, source_target_pairs={{0,24},{8,16},{16,8},{24,0},{1,25},{9,17},{17,9},{25,1},{2,26},{10... | collective-permute-start | bytes 221192 | tf_op jit(solution)/shard_map/ppermute | solution.py:64
  129.9 5.8 %collective-permute-start.30 = (bf16[288,128]{1,0:T(8,128)(2,1)S(1)}, bf16[288,128]{1,0:T(8,128)(2,1)S(1)}, u32[]{:S(2)}, u32[]{:S(2)}) collective-permute-start(bf16[288,128]{1,0:T(8,128)(2,1)S(1)} %get-tuple-element.33.refs_0_), channel_id=1, source_target_pairs={{0,24},{8,16},{16,8},{24,0},{1,25},{9,17},{17,9},{25,1},{2,26},{10... | collective-permute-start | bytes 221192 | tf_op jit(solution)/shard_map/ppermute | solution.py:64
  (40 other events, 88.4 us)
where the time goes:
time: 141 us; the launch traced here: 139 us
  waiting for transfers between devices  57.1 us (40%)
  starting transfers between devices  40.8 us (29%)
  local copies, waits for them, and re-layouts  23.9 us (17%)
  Pallas kernels  13.8 us (10%)
  other arithmetic  2.82 us (2%)
    ppermute x3, waiting for transfers between devices, shift_chips(): return lax.ppermute(array, 'tp', pairs)  29.9 us
    unnamed x63, local copies, waits for them, and re-layouts  23.1 us
    ppermute x12, waiting for transfers between devices, flip_dom(): return lax.ppermute(array, 'dom', [(i, i ^ mask) for i in range(count)])  18.6 us
    ppermute x12, starting transfers between devices, flip_dom(): return lax.ppermute(array, 'dom', [(i, i ^ mask) for i in range(count)])  14.5 us
    ppermute x16, starting transfers between devices, flip_tp(): return lax.ppermute(array, 'tp', [(t, t ^ mask) for t in range(count)])  9.8 us
    all_to_all x2, starting transfers between devices, swap_blocks(): return lax.all_to_all(array, axis, split_axis=0, concat_axis=0, tiled=True)  9.77 us
    ppermute x16, waiting for transfers between devices, flip_tp(): return lax.ppermute(array, 'tp', [(t, t ^ mask) for t in range(count)])  8.66 us
    ppermute x3, starting transfers between devices, shift_chips(): return lax.ppermute(array, 'tp', pairs)  6.75 us
  transfers between devices with their start and end apart: 33, of which 12 were waited for; matrix products, arithmetic and copies ran while one was open for 3% of the time, Pallas kernels for 3%

commit v1 on v0

v1 whole, which is shorter than its diff:
```python
import functools
import math

import jax
import jax.numpy as jnp
from jax import lax
from jax.experimental import pallas as pl
from jax.experimental.pallas import tpu as pltpu
from jax.sharding import PartitionSpec as P


root_three = math.sqrt(3.0)
root_five = math.sqrt(5.0)
root_fifteen = math.sqrt(15.0)
cutoff_radius = 6.0
parts = 9
env_factor = 0.25
lanes = 128
cores = 2
bf16 = jnp.bfloat16
f32 = jnp.float32


mib = 1024 * 1024
in_vmem = pl.BlockSpec(memory_space=pltpu.VMEM)
in_smem = pl.BlockSpec(memory_space=pltpu.SMEM)
in_hbm = pl.BlockSpec(memory_space=pltpu.HBM)
anywhere = pl.BlockSpec(memory_space=pl.ANY)


def harmonics(vectors):
    along_x = vectors[0]
    along_y = vectors[1]
    along_z = vectors[2]
    radius = jnp.sqrt(along_x * along_x + along_y * along_y + along_z * along_z)
    unit_x = along_x / radius
    unit_y = along_y / radius
    unit_z = along_z / radius
    ratio = radius / cutoff_radius
    envelope = (1.0 - ratio * ratio) ** 2
    factors = [
        jnp.ones_like(unit_x),
        root_three * unit_x,
        root_three * unit_y,
        root_three * unit_z,
        root_fifteen * unit_x * unit_y,
        root_fifteen * unit_y * unit_z,
        root_five / 2.0 * (3.0 * unit_z * unit_z - 1.0),
        root_fifteen * unit_x * unit_z,
        root_fifteen / 2.0 * (unit_x * unit_x - unit_y * unit_y),
    ]
    return [factor * envelope for factor in factors]


def contract_rows(left, right):
    return lax.dot_general(
        left, right, (((0,), (0,)), ((), ())), preferred_element_type=f32
    )


def swap_blocks(array, axis):
    return lax.all_to_all(array, axis, split_axis=0, concat_axis=0, tiled=True)


def flip_dom(array, mask):
    count = lax.axis_size("dom")
    return lax.ppermute(array, "dom", [(i, i ^ mask) for i in range(count)])


def shift_chips(array, step):
    count = lax.axis_size("tp")
    chips = count // cores
    pairs = [(t, (t // cores + step) % chips * cores + t % cores) for t in range(count)]
    return lax.ppermute(array, "tp", pairs)


def flip_tp(array, mask):
    count = lax.axis_size("tp")
    return lax.ppermute(array, "tp", [(t, t ^ mask) for t in range(count)])


def other_core(array):
    return flip_tp(array, 1)


def stay(array):
    return pltpu.with_memory_space_constraint(array, pltpu.HBM)


def grant(size):
    return pltpu.CompilerParams(vmem_limit_bytes=size * mib)


def prepare_kernel(*refs):
    sources, (full_ref, own_ref), held, sems = refs[:3], refs[3:5], refs[5:8], refs[8]
    copies = [
        pltpu.make_async_copy(source, place, sems.at[i])
        for i, (source, place) in enumerate(zip(sources, held))
    ]
    for copy in copies:
        copy.start()
    first_ref, second_ref, env_ref = held
    quarters = full_ref.shape[0]
    width = first_ref.shape[0] // quarters
    chan = env_ref.shape[1] // quarters
    copies[0].wait()
    for q in range(quarters):
        for i in range(width // lanes):
            start = q * width + i * lanes
            full_ref[q, i * lanes : (i + 1) * lanes, :] = first_ref[start : start + lanes, :].T
    copies[1].wait()
    for q in range(quarters):
        full_ref[q, width : 2 * width, :] = second_ref[:, q * width : (q + 1) * width].T
    copies[2].wait()
    for q in range(quarters):
        full_ref[q, 2 * width :, :] = env_ref[:, q * chan : (q + 1) * chan].T
    own_ref[...] = full_ref[lax.axis_index("dom")]


def mlp_kernel(x_ref, *refs, quarters, chips, chan, batches):
    per_group = 1 + len(batches) * quarters
    sources = [refs[g * per_group : (g + 1) * per_group] for g in range(cores)]
    shards, depth, _ = x_ref.shape
    outs = refs[cores * per_group :]
    new_refs, outs = outs[:shards], outs[shards:]
    out_ref, first, second, env, moved, hidden, fresh, rows_out, sems = outs
    total = shards * depth
    width = total // quarters
    per_quarter = shards // quarters
    dom, place = lax.axis_index("dom"), lax.axis_index("tp")
    chip, core = place // cores, lax.rem(place, cores)
    for j in range(quarters):
        for i in range(per_quarter):
            start = j * width + i * depth
            moved[start : start + depth, :] = x_ref[(dom ^ j) * per_quarter + i]
    order = [(0, None, 0)]
    for batch, steps in enumerate(batches):
        order += [(k, batch, at) for at, k in enumerate(steps)]
    for k, batch, within in order:
        for g in range(cores):
            at = (k * cores + g) * depth
            for j in range(quarters):
                if batch is None:
                    block = sources[g][0].at[dom ^ j]
                else:
                    block = sources[g][1 + batch * quarters + j].at[within]
                for i in range(width // lanes):
                    column = j * width + i * lanes
                    first[at : at + depth, column : column + lanes] = block[
                        i * depth : (i + 1) * depth, :
                    ]
                row = width // lanes * depth
                start = pl.multiple_of((dom ^ j) * width, lanes)
                second[pl.ds(start, width), at : at + depth] = block[row : row + width, :]
                row += width
                start = pl.multiple_of((dom ^ j) * chan, chan)
                env[pl.ds(start, chan), at : at + depth] = block[row : row + chan, :]
    value = jnp.dot(first[...], moved[...], preferred_element_type=f32)
    hidden[...] = (value / (1.0 + jnp.exp(-value))).astype(bf16)
    update = jnp.dot(second[...], hidden[...], preferred_element_type=f32)
    for s in range(shards):
        rows = slice(s * depth, (s + 1) * depth)
        fresh[s] = (x_ref[s].astype(f32) + update[rows, :]).astype(bf16)
    copies = [
        pltpu.make_async_copy(fresh.at[place ^ s], out, sems.at[s])
        for s, out in enumerate(new_refs)
    ]
    for copy in copies:
        copy.start()
    for k in range(chips):
        for g in range(cores):
            at = (k * cores + g) * depth
            source = lax.rem(chip + chips - k, chips) * cores + (core if g == 0 else 1 - core)
            moved[at : at + depth, :] = fresh[source]
    rows = jnp.dot(env[...], moved[...], preferred_element_type=f32).astype(bf16)
    per = rows.shape[0] // shards
    for s in range(shards):
        rows_out[s] = rows[s * per : (s + 1) * per, :]
    copies.append(pltpu.make_async_copy(rows_out, out_ref, sems.at[shards]))
    copies[-1].start()
    for copy in copies:
        copy.wait()


def split_kernel(x_ref, tie_ref, out_ref, held, sems_in, sems_out):
    shards, _, edges = held.shape
    arriving = [
        pltpu.make_async_copy(x_ref.at[:, pl.ds(s * edges, edges)], held.at[s], sems_in.at[s])
        for s in range(shards)
    ]
    leaving = [
        pltpu.make_async_copy(held.at[s], out_ref.at[s], sems_out.at[s]) for s in range(shards)
    ]
    for copy in arriving:
        copy.start()
    for before, after in zip(arriving, leaving):
        before.wait()
        after.start()
    for copy in leaving:
        copy.wait()


def join_kernel(tie_ref, *refs):
    pieces, out_ref = refs[:-1], refs[-1]
    edges = pieces[0].shape[1]
    for s, piece in enumerate(pieces):
        at = pl.multiple_of((lax.axis_index("tp") ^ s) * edges, lanes)
        out_ref[:, pl.ds(at, edges)] = piece[...]


def join_pieces(back, tie):
    depth, edges = back[0].shape
    return pl.pallas_call(
        join_kernel,
        out_shape=jax.ShapeDtypeStruct((depth, edges * len(back)), bf16),
        in_specs=[anywhere] + [in_vmem] * len(back),
        out_specs=in_vmem,
        compiler_params=grant(8),
        name="join",
    )(tie, *back)


def spread_mlp(latent, w_first, w_second, w_env, ties):
    domains = lax.axis_size("dom")
    shards = lax.axis_size("tp")
    chips = shards // cores
    total = w_first.shape[0]
    depth = w_first.shape[1]
    channels = w_env.shape[1]
    width = total // domains
    chan = channels // domains
    rows = 2 * width + chan
    edges = latent.shape[1] // shards
    full, own = pl.pallas_call(
        prepare_kernel,
        out_shape=(
            jax.ShapeDtypeStruct((domains, rows, depth), bf16),
            jax.ShapeDtypeStruct((rows, depth), bf16),
        ),
        in_specs=[in_hbm] * 3,
        out_specs=(in_vmem, in_vmem),
        scratch_shapes=[pltpu.VMEM(w.shape, bf16) for w in (w_first, w_second, w_env)]
        + [pltpu.SemaphoreType.DMA((3,))],
        compiler_params=grant(8),
        name="prepare",
    )(stay(w_first), stay(w_second), stay(w_env))
    pieces = pl.pallas_call(
        split_kernel,
        out_shape=pltpu.HBM((shards, depth, edges), bf16),
        in_specs=[in_hbm, anywhere],
        out_specs=in_hbm,
        scratch_shapes=[pltpu.VMEM((shards, depth, edges), bf16)]
        + [pltpu.SemaphoreType.DMA((shards,))] * 2,
        compiler_params=grant(8),
        name="split",
    )(stay(latent), own)
    shifted = {k: shift_chips(own, k) for k in range(1, chips)}
    edge_rows = swap_blocks(pieces, "tp")
    edge_rows, *ties = lax.optimization_barrier((edge_rows, *ties))
    near = [k for k in (1, chips - 1)]
    batches = [near, [k for k in range(2, chips - 1)]]
    mine = [full]
    for steps in batches:
        arrived = jnp.stack([shifted[k] for k in steps])
        mine += [arrived] + [flip_dom(arrived, j) for j in range(1, domains)]
    others = [other_core(array) for array in mine]
    *new_rows, weight_rows = pl.pallas_call(
        functools.partial(mlp_kernel, quarters=domains, chips=chips, chan=chan, batches=batches),
        out_shape=[pltpu.HBM((depth, edges), bf16)] * shards
        + [pltpu.HBM((shards, channels // shards, edges), bf16)],
        in_specs=[in_vmem] * (1 + 2 * len(mine)),
        out_specs=[in_hbm] * (shards + 1),
        scratch_shapes=[
            pltpu.VMEM((total, total), bf16),
            pltpu.VMEM((total, total), bf16),
            pltpu.VMEM((channels, total), bf16),
            pltpu.VMEM((total, edges), bf16),
            pltpu.VMEM((total, edges), bf16),
            pltpu.VMEM((shards, depth, edges), bf16),
            pltpu.VMEM((shards, channels // shards, edges), bf16),
            pltpu.SemaphoreType.DMA((shards + 1,)),
        ],
        compiler_params=grant(28),
        name="mlp",
    )(edge_rows, *mine, *others)
    weights = swap_blocks(weight_rows, "tp")
    back = [new_rows[0]] + [flip_tp(new_rows[s], s) for s in range(1, shards)]
    return (lambda tie: join_pieces(back, tie)), weights, ties


def gathered_mlp(latent, w_first, w_second, w_env, ties):
    edge_rows = lax.all_to_all(latent, "tp", split_axis=1, concat_axis=0, tiled=True)
    full_first = lax.all_gather(w_first, "tp", axis=1, tiled=True)
    full_second = lax.all_gather(w_second, "tp", axis=0, tiled=True)
    full_env = lax.all_gather(w_env, "tp", axis=0, tiled=True)
    hidden = jax.nn.silu(contract_rows(full_first, edge_rows)).astype(bf16)
    update = contract_rows(full_second, hidden)
    new_rows = (edge_rows.astype(f32) + update).astype(bf16)
    weight_rows = contract_rows(full_env, new_rows).astype(bf16)
    shards = lax.axis_size("tp")
    weights = swap_blocks(weight_rows.reshape(shards, -1, weight_rows.shape[1]), "tp")
    new_rows, weights = lax.optimization_barrier((new_rows, weights))
    latent_new = lax.all_to_all(new_rows, "tp", split_axis=0, concat_axis=1, tiled=True)
    return (lambda tie: latent_new), weights, ties


def geometry_kernel(vec_ref, fill_ref, centers_ref, out_ref):
    vectors = [vec_ref[i] for i in range(3)]
    ids = lax.broadcasted_iota(jnp.int32, vectors[0].shape, 1)
    alive = (ids < fill_ref[...]).astype(f32)
    for m, part in enumerate(harmonics(vectors)):
        out_ref[m] = part * alive
    out_ref[parts] = centers_ref[...].astype(f32)


def select_atoms(h_ref, block, atoms):
    ids = lax.broadcasted_iota(jnp.int32, (atoms, lanes), 0).astype(f32)
    return (ids == h_ref[parts, pl.ds(block, 1), :]).astype(f32).astype(bf16)


def sums_kernel(dest_ref, w_ref, h_ref, *refs):
    outs, total = refs[:-1], refs[-1]
    shards, _, edges = w_ref.shape
    atoms = total.shape[2]
    per = edges // lanes
    total[...] = jnp.zeros_like(total)

    def step(s, carry):
        for i in range(per):
            block = s * per + i
            weight = w_ref[s, :, i * lanes : (i + 1) * lanes].astype(f32)
            terms = [
                (h_ref[m, pl.ds(block, 1), :] * weight).astype(bf16) for m in range(parts)
            ]
            contrib = jnp.concatenate(terms, axis=0)
            chosen = select_atoms(h_ref, block, atoms)
            slot = dest_ref[block] ^ lax.axis_index("dom")
            total[slot] += lax.dot_general(
                contrib, chosen, (((1,), (1,)), ((), ())), preferred_element_type=f32
            )
        return carry

    lax.fori_loop(0, shards, step, 0)
    for j, out in enumerate(outs):
        out[...] = total[j].astype(out.dtype)


def invariants_kernel(dest_ref, w_ref, h_ref, *refs):
    domains = len(refs) - 3
    out_ref, token_ref, env = refs[domains:]
    token_ref[...] = jnp.zeros_like(token_ref)
    shards, chan, edges = w_ref.shape
    atoms = env.shape[2]
    per = edges // lanes
    for j in range(domains):
        env[j] = refs[j][...]

    def step(s, carry):
        for i in range(per):
            block = s * per + i
            weight = w_ref[s, :, i * lanes : (i + 1) * lanes].astype(f32)
            chosen = select_atoms(h_ref, block, atoms)
            slot = dest_ref[block] ^ lax.axis_index("dom")
            found = jnp.dot(env[slot], chosen, preferred_element_type=f32)
            products = [
                found[m * chan : (m + 1) * chan, :] * h_ref[m, pl.ds(block, 1), :]
                for m in range(parts)
            ]
            at = pl.multiple_of(block * lanes, lanes)
            out_ref[0, :, pl.ds(at, lanes)] = products[0] * weight
            out_ref[1, :, pl.ds(at, lanes)] = sum(products[2:4], products[1]) * weight
            out_ref[2, :, pl.ds(at, lanes)] = sum(products[5:9], products[4]) * weight
        return carry

    lax.fori_loop(0, shards, step, 0)


def on_device(
    latent,
    w_first,
    w_second,
    w_env,
    edge_vec,
    centers,
    block_dest,
    block_fill,
    species,
    species_gain,
):
    domains = lax.axis_size("dom")
    shards = lax.axis_size("tp")
    nblocks = block_fill.shape[0]
    atoms = species.shape[0]
    chan = species_gain.shape[1]
    depth, edges = latent.shape
    spread = (
        depth == lanes
        and w_first.shape[0] % (domains * lanes) == 0
        and w_env.shape[1] % (domains * 16) == 0
        and shards % cores == 0
        and shards // cores >= 4
    )
    harmonic = pl.pallas_call(
        geometry_kernel,
        out_shape=jax.ShapeDtypeStruct((parts + 1, nblocks, lanes), f32),
        in_specs=[in_vmem] * 3,
        out_specs=in_vmem,
        compiler_params=grant(4),
        name="geometry",
    )(edge_vec.reshape(3, nblocks, lanes), block_fill[:, None], centers.reshape(nblocks, lanes))
    target = stay(block_dest[:, 0])
    species_ids = jnp.arange(species_gain.shape[0], dtype=jnp.int32)
    gain_sel = jnp.sum(
        jnp.where(
            species[None, None, :] == species_ids[:, None, None], species_gain[:, :, None], 0.0
        ),
        axis=0,
    )
    mlp = spread_mlp if spread else gathered_mlp
    finish, weights, (harmonic, gain_sel) = mlp(
        latent, w_first, w_second, w_env, (harmonic, gain_sel)
    )

    rows = parts * chan
    sums = pl.pallas_call(
        sums_kernel,
        out_shape=[jax.ShapeDtypeStruct((rows, atoms), f32)]
        + [jax.ShapeDtypeStruct((rows, atoms), bf16)] * (domains - 1),
        in_specs=[in_smem] + [in_vmem] * 2,
        out_specs=[in_vmem] * domains,
        scratch_shapes=[pltpu.VMEM((domains, rows, atoms), f32)],
        compiler_params=grant(8),
        name="sums",
    )(target, weights, harmonic)
    env_raw = sums[0]
    for j in range(1, domains):
        env_raw = env_raw + flip_dom(sums[j], j).astype(f32)
    env_out = env_raw.reshape(parts, chan, atoms) * gain_sel[None, :, :] * env_factor
    env_half = env_out.astype(bf16).reshape(rows, atoms)
    looked = [env_half] + [flip_dom(env_half, j) for j in range(1, domains)]
    invariants, token = pl.pallas_call(
        invariants_kernel,
        out_shape=(
            jax.ShapeDtypeStruct((3, chan, edges), f32),
            jax.ShapeDtypeStruct((8, lanes), f32),
        ),
        in_specs=[in_smem] + [in_vmem] * (2 + domains),
        out_specs=(in_vmem, in_vmem),
        scratch_shapes=[pltpu.VMEM((domains, rows, atoms), bf16)],
        compiler_params=grant(10),
        name="invariants",
    )(target, weights, harmonic, *looked)
    return (finish(token), env_out, invariants)


def solution(mesh):
    in_specs = (
        P("tp", "dom"),
        P(None, "tp"),
        P("tp", None),
        P("tp", None),
        P(None, "dom"),
        P("dom"),
        P("dom", None),
        P("dom"),
        P("dom"),
        P(None, "tp"),
    )
    out_specs = (P("tp", "dom"), P(None, "tp", "dom"), P(None, "tp", "dom"))

    return jax.shard_map(on_device, mesh=mesh, in_specs=in_specs, out_specs=out_specs, check_vma=False)
```

time: 141 us -> 138 us (0.979)
  the two profiles are of different devices: /device:TPU:0 before, /device:TPU:9 now
where the time goes in v1:
time: 138 us; the launch traced here: 137 us
  waiting for transfers between devices  61.2 us (44%)
  starting transfers between devices  37.4 us (27%)
  Pallas kernels  17 us (12%)
  blocking collectives  13.2 us (10%)
  local copies, waits for them, and re-layouts  6.69 us (5%)
    ppermute x3, waiting for transfers between devices, shift_chips(): return lax.ppermute(array, 'tp', pairs)  30.1 us
    ppermute x16, waiting for transfers between devices, flip_tp(): return lax.ppermute(array, 'tp', [(t, t ^ mask) for t in range(count)])  18.7 us
    ppermute x16, starting transfers between devices, flip_tp(): return lax.ppermute(array, 'tp', [(t, t ^ mask) for t in range(count)])  18.5 us
    all_to_all x1, blocking collectives, swap_blocks(): return lax.all_to_all(array, axis, split_axis=0, concat_axis=0, tiled=True)  13.2 us
    ppermute x12, waiting for transfers between devices, flip_dom(): return lax.ppermute(array, 'dom', [(i, i ^ mask) for i in range(count)])  12.4 us
    ppermute x12, starting transfers between devices, flip_dom(): return lax.ppermute(array, 'dom', [(i, i ^ mask) for i in range(count)])  10.8 us
    unnamed x43, local copies, waits for them, and re-layouts  6.6 us
    pallas_call x1, Pallas kernels, spread_mlp(): pl.pallas_call(functools.partial(mlp_kernel, quarters=domains, chips=chip...  5.91 us
  transfers between devices with their start and end apart: 32, of which 12 were waited for; matrix products, arithmetic and copies ran while one was open for 1% of the time, Pallas kernels for 3%

profile of v1, /device:TPU:9, one launch (start us, length us, event | category | flops | bytes accessed | tf_op | source)
XLA Modules:
  0.0 137.2 jit_solution(1077555011220813048)
XLA Ops:
  2.0 2.1 %split.1 = bf16[8,128,512]{2,1,0:T(8,128)(2,1)} custom-call(bf16[128,4096]{1,0:T(8,128)(2,1)} %x_ref.1, bf16[576,128]{1,0:T(8,128)(2,1)S(1)} %get-tuple-element.23.tie_ref), custom_call_target="tpu_custom_call" | custom-call | tf_op jit(solution)/shard_map/split/pallas_call | solution.py:247
  4.2 5.7 %all-to-all-start = ((bf16[8,128,512]{2,1,0:T(8,128)(2,1)}), bf16[8,128,512]{2,1,0:T(8,128)(2,1)S(1)}, u32[]{:S(2)}, u32[]{:S(2)}) async-start(bf16[8,128,512]{2,1,0:T(8,128)(2,1)} %split.1), calls=%async_computation | async-start | bytes 2097152 | tf_op jit(solution)/shard_map/all_to_all | solution.py:62
  9.9 2.1 %collective-permute-start.5 = (bf16[576,128]{1,0:T(8,128)(2,1)S(1)}, bf16[576,128]{1,0:T(8,128)(2,1)S(1)}, u32[]{:S(2)}, u32[]{:S(2)}) collective-permute-start(bf16[576,128]{1,0:T(8,128)(2,1)S(1)} %get-tuple-element.23.tie_ref), channel_id=1, source_target_pairs={{0,4},{1,5},{2,6},{3,7},{4,0},{5,1},{6,2},{7,3},{8,12},{9,13},{10,... | collective-permute-start | bytes 442376 | tf_op jit(solution)/shard_map/ppermute | solution.py:74
  12.3 30.1 %collective-permute-done.5 = bf16[576,128]{1,0:T(8,128)(2,1)S(1)} collective-permute-done((bf16[576,128]{1,0:T(8,128)(2,1)S(1)}, bf16[576,128]{1,0:T(8,128)(2,1)S(1)}, u32[]{:S(2)}, u32[]{:S(2)}) %collective-permute-start.5) | collective-permute-done | bytes 147488 | tf_op jit(solution)/shard_map/ppermute | solution.py:74
  42.4 2.2 %collective-permute-start.8 = (bf16[1,576,128]{2,1,0:T(8,128)(2,1)S(1)}, bf16[1,576,128]{2,1,0:T(8,128)(2,1)S(1)}, u32[]{:S(2)}, u32[]{:S(2)}) collective-permute-start(bf16[1,576,128]{2,1,0:T(8,128)(2,1)S(1)} %bitcast.18), channel_id=1, source_target_pairs={{0,24},{8,16},{16,8},{24,0},{1,25},{9,17},{17,9},{25,1},{2,26},{10... | collective-permute-start | bytes 442376 | tf_op jit(solution)/shard_map/ppermute | solution.py:67
  46.1 2.1 %collective-permute-done.8.refs_8_ = bf16[1,576,128]{2,1,0:T(8,128)(2,1)S(1)} collective-permute-done((bf16[1,576,128]{2,1,0:T(8,128)(2,1)S(1)}, bf16[1,576,128]{2,1,0:T(8,128)(2,1)S(1)}, u32[]{:S(2)}, u32[]{:S(2)}) %collective-permute-start.8) | collective-permute-done | bytes 147488 | tf_op jit(solution)/shard_map/ppermute | solution.py:67
  48.2 1.4 %collective-permute-start.17 = (bf16[1,576,128]{2,1,0:T(8,128)(2,1)S(1)}, bf16[1,576,128]{2,1,0:T(8,128)(2,1)S(1)}, u32[]{:S(2)}, u32[]{:S(2)}) collective-permute-start(bf16[1,576,128]{2,1,0:T(8,128)(2,1)S(1)} %collective-permute-done.8.refs_8_), channel_id=1, source_target_pairs={{0,1},{1,0},{2,3},{3,2},{4,5},{5,4},{6,7},{7,6},{8,9},{9,8},{10,11... | collective-permute-start | bytes 442376 | tf_op jit(solution)/shard_map/ppermute | solution.py:79
  49.6 2.7 %collective-permute-done.7.refs_7_ = bf16[1,576,128]{2,1,0:T(8,128)(2,1)S(1)} collective-permute-done((bf16[1,576,128]{2,1,0:T(8,128)(2,1)S(1)}, bf16[1,576,128]{2,1,0:T(8,128)(2,1)S(1)}, u32[]{:S(2)}, u32[]{:S(2)}) %collective-permute-start.7) | collective-permute-done | bytes 147488 | tf_op jit(solution)/shard_map/ppermute | solution.py:67
  52.7 1.5 %collective-permute-start.4 = (bf16[2,576,128]{2,1,0:T(8,128)(2,1)S(1)}, bf16[2,576,128]{2,1,0:T(8,128)(2,1)S(1)}, u32[]{:S(2)}, u32[]{:S(2)}) collective-permute-start(bf16[2,576,128]{2,1,0:T(8,128)(2,1)S(1)} %pad_maximum_fusion.refs_1_), channel_id=1, source_target_pairs={{0,24},{8,16},{16,8},{24,0},{1,25},{9,17},{17,9},{25,1},{2,26},{10... | collective-permute-start | bytes 884744 | tf_op jit(solution)/shard_map/ppermute | solution.py:67
  58.6 1.5 %collective-permute-done.15.refs_15_ = bf16[1,576,128]{2,1,0:T(8,128)(2,1)} collective-permute-done((bf16[1,576,128]{2,1,0:T(8,128)(2,1)}, bf16[1,576,128]{2,1,0:T(8,128)(2,1)}, u32[]{:S(2)}, u32[]{:S(2)}) %collective-permute-start.15) | collective-permute-done | bytes 147488 | tf_op jit(solution)/shard_map/ppermute | solution.py:79
  60.3 1.9 %collective-permute-done.4.refs_4_ = bf16[2,576,128]{2,1,0:T(8,128)(2,1)S(1)} collective-permute-done((bf16[2,576,128]{2,1,0:T(8,128)(2,1)S(1)}, bf16[2,576,128]{2,1,0:T(8,128)(2,1)S(1)}, u32[]{:S(2)}, u32[]{:S(2)}) %collective-permute-start.4) | collective-permute-done | bytes 294944 | tf_op jit(solution)/shard_map/ppermute | solution.py:67
  62.2 1.6 %collective-permute-start.13 = (bf16[2,576,128]{2,1,0:T(8,128)(2,1)S(1)}, bf16[2,576,128]{2,1,0:T(8,128)(2,1)}, u32[]{:S(2)}, u32[]{:S(2)}) collective-permute-start(bf16[2,576,128]{2,1,0:T(8,128)(2,1)S(1)} %collective-permute-done.4.refs_4_), channel_id=1, source_target_pairs={{0,1},{1,0},{2,3},{3,2},{4,5},{5,4},{6,7},{7,6},{8,9},{9,8},{10,11... | collective-permute-start | bytes 884744 | tf_op jit(solution)/shard_map/ppermute | solution.py:79
  63.7 5.3 %collective-permute-done.3.refs_3_ = bf16[2,576,128]{2,1,0:T(8,128)(2,1)S(1)} collective-permute-done((bf16[2,576,128]{2,1,0:T(8,128)(2,1)S(1)}, bf16[2,576,128]{2,1,0:T(8,128)(2,1)S(1)}, u32[]{:S(2)}, u32[]{:S(2)}) %collective-permute-start.3) | collective-permute-done | bytes 294944 | tf_op jit(solution)/shard_map/ppermute | solution.py:67
  75.9 5.9 %mlp.1 = (bf16[128,512]{1,0:T(8,128)(2,1)}, bf16[128,512]{1,0:T(8,128)(2,1)}, bf16[128,512]{1,0:T(8,128)(2,1)}, bf16[128,512]{1,0:T(8,128)(2,1)}, bf16[128,512]{...) custom-call(bf16[8,128,512]{2,1,0:T(8,128)(2,1)S(1)} %all-to-all-don, ...), custom_call_target="tpu_custom_call" | custom-call | tf_op jit(solution)/shard_map/mlp/pallas_call | solution.py:267
  81.9 13.2 %all_to_all.10.w_ref = bf16[8,32,512]{2,1,0:T(8,128)(2,1)S(1)} all-to-all(bf16[8,32,512]{2,1,0:T(8,128)(2,1)} %get-tuple-element.26), channel_id=1, replica_groups=mesh['dom'=4,'tp'=8] {'tp'}, dimensions={0} | all-to-all | bytes 524288 | tf_op jit(solution)/shard_map/all_to_all | solution.py:62
  95.1 2.8 %sums.1 = (f32[288,128]{1,0:T(8,128)S(1)}, bf16[288,128]{1,0:T(8,128)(2,1)S(1)}, bf16[288,128]{1,0:T(8,128)(2,1)S(1)}, bf16[288,128]{1,0:T(8,128)(2,1)S(1)}) custom-call(s32[32]{0:T(128)} %bitcast.28, bf16[8,32,512]{2,1,0:T(8,128)(2,1)S(1)} %all_to_all.10.w_ref, f32[10,32,128]{2,1,0:T(8,128)S(1)} %geometry.1.h_ref), custom_call_target="tpu_custom_call" | custom-call | tf_op jit(solution)/shard_map/sums/pallas_call | solution.py:425
  100.6 1.9 %collective-permute-start.24 = (bf16[128,512]{1,0:T(8,128)(2,1)}, bf16[128,512]{1,0:T(8,128)(2,1)S(1)}, u32[]{:S(2)}, u32[]{:S(2)}) collective-permute-start(bf16[128,512]{1,0:T(8,128)(2,1)} %get-tuple-element.35), channel_id=1, source_target_pairs={{0,1},{1,0},{2,3},{3,2},{4,5},{5,4},{6,7},{7,6},{8,9},{9,8},{10,11... | collective-permute-start | bytes 393224 | tf_op jit(solution)/shard_map/ppermute | solution.py:79
  102.5 1.7 %collective-permute-start.25 = (bf16[128,512]{1,0:T(8,128)(2,1)}, bf16[128,512]{1,0:T(8,128)(2,1)S(1)}, u32[]{:S(2)}, u32[]{:S(2)}) collective-permute-start(bf16[128,512]{1,0:T(8,128)(2,1)} %get-tuple-element.36), channel_id=1, source_target_pairs={{0,2},{1,3},{2,0},{3,1},{4,6},{5,7},{6,4},{7,5},{8,10},{9,11},{10,... | collective-permute-start | bytes 393224 | tf_op jit(solution)/shard_map/ppermute | solution.py:79
  107.3 4.5 %collective-permute-start.26 = (bf16[128,512]{1,0:T(8,128)(2,1)S(1)}, bf16[128,512]{1,0:T(8,128)(2,1)S(1)}, u32[]{:S(2)}, u32[]{:S(2)}) collective-permute-start(bf16[128,512]{1,0:T(8,128)(2,1)S(1)} %copy-done.19), channel_id=1, source_target_pairs={{0,3},{1,2},{2,1},{3,0},{4,7},{5,6},{6,5},{7,4},{8,11},{9,10},{10,... | collective-permute-start | bytes 393224 | tf_op jit(solution)/shard_map/ppermute | solution.py:79
  111.8 1.6 %collective-permute-start.28 = (bf16[128,512]{1,0:T(8,128)(2,1)S(1)}, bf16[128,512]{1,0:T(8,128)(2,1)S(1)}, u32[]{:S(2)}, u32[]{:S(2)}) collective-permute-start(bf16[128,512]{1,0:T(8,128)(2,1)S(1)} %copy-done.17), channel_id=1, source_target_pairs={{0,5},{1,4},{2,7},{3,6},{4,1},{5,0},{6,3},{7,2},{8,13},{9,12},{10,... | collective-permute-start | bytes 393224 | tf_op jit(solution)/shard_map/ppermute | solution.py:79
  116.8 3.7 %invariants.1 = (f32[3,32,4096]{2,1,0:T(8,128)}, f32[8,128]{1,0:T(8,128)S(1)}) custom-call(s32[32]{0:T(128)} %bitcast.29, bf16[8,32,512]{2,1,0:T(8,128)(2,1)S(1)} %all_to_all.10.w_ref, f32[10,32,128]{2,1,0:T(8,128)S(1)} %geometry.1.h_ref, bf16[288,128]{1,0:T(8,128)(2,1)S(1)} %get-tuple-element.43.refs_0_, ...), custom_call_target="tpu_custom_call" | custom-call | tf_op jit(solution)/shard_map/invariants/pallas_call | solution.py:441
  120.6 8.1 %collective-permute-done.28.refs_5_ = bf16[128,512]{1,0:T(8,128)(2,1)S(1)} collective-permute-done((bf16[128,512]{1,0:T(8,128)(2,1)S(1)}, bf16[128,512]{1,0:T(8,128)(2,1)S(1)}, u32[]{:S(2)}, u32[]{:S(2)}) %collective-permute-start.28) | collective-permute-done | bytes 131104 | tf_op jit(solution)/shard_map/ppermute | solution.py:79
  128.7 4.1 %collective-permute-done.29.refs_6_ = bf16[128,512]{1,0:T(8,128)(2,1)S(1)} collective-permute-done((bf16[128,512]{1,0:T(8,128)(2,1)S(1)}, bf16[128,512]{1,0:T(8,128)(2,1)S(1)}, u32[]{:S(2)}, u32[]{:S(2)}) %collective-permute-start.29) | collective-permute-done | bytes 131104 | tf_op jit(solution)/shard_map/ppermute | solution.py:79
  132.8 3.4 %collective-permute-done.30.refs_7_ = bf16[128,512]{1,0:T(8,128)(2,1)S(1)} collective-permute-done((bf16[128,512]{1,0:T(8,128)(2,1)S(1)}, bf16[128,512]{1,0:T(8,128)(2,1)S(1)}, u32[]{:S(2)}, u32[]{:S(2)}) %collective-permute-start.30) | collective-permute-done | bytes 131104 | tf_op jit(solution)/shard_map/ppermute | solution.py:79
  (97 shorter events, 25.3 us)
Async XLA Ops:
  4.2 65.6 %all-to-all-start = ((bf16[8,128,512]{2,1,0:T(8,128)(2,1)}), bf16[8,128,512]{2,1,0:T(8,128)(2,1)S(1)}, u32[]{:S(2)}, u32[]{:S(2)}) async-start(bf16[8,128,512]{2,1,0:T(8,128)(2,1)} %split.1), calls=%async_computation | async-start | bytes 2097152 | tf_op jit(solution)/shard_map/all_to_all | solution.py:62
  9.9 32.4 %collective-permute-start.5 = (bf16[576,128]{1,0:T(8,128)(2,1)S(1)}, bf16[576,128]{1,0:T(8,128)(2,1)S(1)}, u32[]{:S(2)}, u32[]{:S(2)}) collective-permute-start(bf16[576,128]{1,0:T(8,128)(2,1)S(1)} %get-tuple-element.23.tie_ref), channel_id=1, source_target_pairs={{0,4},{1,5},{2,6},{3,7},{4,0},{5,1},{6,2},{7,3},{8,12},{9,13},{10,... | collective-permute-start | bytes 442376 | tf_op jit(solution)/shard_map/ppermute | solution.py:74
  12.0 33.8 %collective-permute-start.1 = (bf16[576,128]{1,0:T(8,128)(2,1)S(1)}, bf16[576,128]{1,0:T(8,128)(2,1)S(1)}, u32[]{:S(2)}, u32[]{:S(2)}) collective-permute-start(bf16[576,128]{1,0:T(8,128)(2,1)S(1)} %get-tuple-element.23.tie_ref), channel_id=1, source_target_pairs={{0,6},{1,7},{2,0},{3,1},{4,2},{5,3},{6,4},{7,5},{8,14},{9,15},{10,... | collective-permute-start | bytes 442376 | tf_op jit(solution)/shard_map/ppermute | solution.py:74
  44.5 7.8 %collective-permute-start.7 = (bf16[1,576,128]{2,1,0:T(8,128)(2,1)S(1)}, bf16[1,576,128]{2,1,0:T(8,128)(2,1)S(1)}, u32[]{:S(2)}, u32[]{:S(2)}) collective-permute-start(bf16[1,576,128]{2,1,0:T(8,128)(2,1)S(1)} %bitcast.19), channel_id=1, source_target_pairs={{0,16},{8,24},{16,0},{24,8},{1,17},{9,25},{17,1},{25,9},{2,18},{10... | collective-permute-start | bytes 442376 | tf_op jit(solution)/shard_map/ppermute | solution.py:67
  44.8 7.9 %collective-permute-start = (bf16[576,128]{1,0:T(8,128)(2,1)S(1)}, bf16[576,128]{1,0:T(8,128)(2,1)S(1)}, u32[]{:S(2)}, u32[]{:S(2)}) collective-permute-start(bf16[576,128]{1,0:T(8,128)(2,1)S(1)} %get-tuple-element.23.tie_ref), channel_id=1, source_target_pairs={{0,2},{1,3},{2,4},{3,5},{4,6},{5,7},{6,0},{7,1},{8,10},{9,11},{10,... | collective-permute-start | bytes 442376 | tf_op jit(solution)/shard_map/ppermute | solution.py:74
  44.8 9.5 %collective-permute-start.14 = (bf16[1,576,128]{2,1,0:T(8,128)(2,1)S(1)}, bf16[1,576,128]{2,1,0:T(8,128)(2,1)S(1)}, u32[]{:S(2)}, u32[]{:S(2)}) collective-permute-start(bf16[1,576,128]{2,1,0:T(8,128)(2,1)S(1)} %bitcast.20), channel_id=1, source_target_pairs={{0,1},{1,0},{2,3},{3,2},{4,5},{5,4},{6,7},{7,6},{8,9},{9,8},{10,11... | collective-permute-start | bytes 442376 | tf_op jit(solution)/shard_map/ppermute | solution.py:79
  45.8 10.0 %collective-permute-start.6 = (bf16[1,576,128]{2,1,0:T(8,128)(2,1)S(1)}, bf16[1,576,128]{2,1,0:T(8,128)(2,1)}, u32[]{:S(2)}, u32[]{:S(2)}) collective-permute-start(bf16[1,576,128]{2,1,0:T(8,128)(2,1)S(1)} %bitcast.21), channel_id=1, source_target_pairs={{0,8},{8,0},{16,24},{24,16},{1,9},{9,1},{17,25},{25,17},{2,10},{10... | collective-permute-start | bytes 442376 | tf_op jit(solution)/shard_map/ppermute | solution.py:67
  48.2 7.9 %collective-permute-start.17 = (bf16[1,576,128]{2,1,0:T(8,128)(2,1)S(1)}, bf16[1,576,128]{2,1,0:T(8,128)(2,1)S(1)}, u32[]{:S(2)}, u32[]{:S(2)}) collective-permute-start(bf16[1,576,128]{2,1,0:T(8,128)(2,1)S(1)} %collective-permute-done.8.refs_8_), channel_id=1, source_target_pairs={{0,1},{1,0},{2,3},{3,2},{4,5},{5,4},{6,7},{7,6},{8,9},{9,8},{10,11... | collective-permute-start | bytes 442376 | tf_op jit(solution)/shard_map/ppermute | solution.py:79
  52.7 9.4 %collective-permute-start.4 = (bf16[2,576,128]{2,1,0:T(8,128)(2,1)S(1)}, bf16[2,576,128]{2,1,0:T(8,128)(2,1)S(1)}, u32[]{:S(2)}, u32[]{:S(2)}) collective-permute-start(bf16[2,576,128]{2,1,0:T(8,128)(2,1)S(1)} %pad_maximum_fusion.refs_1_), channel_id=1, source_target_pairs={{0,24},{8,16},{16,8},{24,0},{1,25},{9,17},{17,9},{25,1},{2,26},{10... | collective-permute-start | bytes 884744 | tf_op jit(solution)/shard_map/ppermute | solution.py:67
  54.9 14.2 %collective-permute-start.3 = (bf16[2,576,128]{2,1,0:T(8,128)(2,1)S(1)}, bf16[2,576,128]{2,1,0:T(8,128)(2,1)S(1)}, u32[]{:S(2)}, u32[]{:S(2)}) collective-permute-start(bf16[2,576,128]{2,1,0:T(8,128)(2,1)S(1)} %pad_maximum_fusion.refs_1_), channel_id=1, source_target_pairs={{0,16},{8,24},{16,0},{24,8},{1,17},{9,25},{17,1},{25,9},{2,18},{10... | collective-permute-start | bytes 884744 | tf_op jit(solution)/shard_map/ppermute | solution.py:67
  55.9 13.6 %collective-permute-start.2 = (bf16[2,576,128]{2,1,0:T(8,128)(2,1)S(1)}, bf16[2,576,128]{2,1,0:T(8,128)(2,1)}, u32[]{:S(2)}, u32[]{:S(2)}) collective-permute-start(bf16[2,576,128]{2,1,0:T(8,128)(2,1)S(1)} %pad_maximum_fusion.refs_1_), channel_id=1, source_target_pairs={{0,8},{8,0},{16,24},{24,16},{1,9},{9,1},{17,25},{25,17},{2,10},{10... | collective-permute-start | bytes 884744 | tf_op jit(solution)/shard_map/ppermute | solution.py:67
  56.8 13.0 %collective-permute-start.9 = (bf16[4,576,128]{2,1,0:T(8,128)(2,1)S(1)}, bf16[4,576,128]{2,1,0:T(8,128)(2,1)S(1)}, u32[]{:S(2)}, u32[]{:S(2)}) collective-permute-start(bf16[4,576,128]{2,1,0:T(8,128)(2,1)S(1)} %get-tuple-element.25.refs_0_), channel_id=1, source_target_pairs={{0,1},{1,0},{2,3},{3,2},{4,5},{5,4},{6,7},{7,6},{8,9},{9,8},{10,11... | collective-permute-start | bytes 1769480 | tf_op jit(solution)/shard_map/ppermute | solution.py:79
  60.1 9.6 %collective-permute-start.10 = (bf16[2,576,128]{2,1,0:T(8,128)(2,1)S(1)}, bf16[2,576,128]{2,1,0:T(8,128)(2,1)}, u32[]{:S(2)}, u32[]{:S(2)}) collective-permute-start(bf16[2,576,128]{2,1,0:T(8,128)(2,1)S(1)} %pad_maximum_fusion.refs_1_), channel_id=1, source_target_pairs={{0,1},{1,0},{2,3},{3,2},{4,5},{5,4},{6,7},{7,6},{8,9},{9,8},{10,11... | collective-permute-start | bytes 884744 | tf_op jit(solution)/shard_map/ppermute | solution.py:79
  62.2 7.6 %collective-permute-start.13 = (bf16[2,576,128]{2,1,0:T(8,128)(2,1)S(1)}, bf16[2,576,128]{2,1,0:T(8,128)(2,1)}, u32[]{:S(2)}, u32[]{:S(2)}) collective-permute-start(bf16[2,576,128]{2,1,0:T(8,128)(2,1)S(1)} %collective-permute-done.4.refs_4_), channel_id=1, source_target_pairs={{0,1},{1,0},{2,3},{3,2},{4,5},{5,4},{6,7},{7,6},{8,9},{9,8},{10,11... | collective-permute-start | bytes 884744 | tf_op jit(solution)/shard_map/ppermute | solution.py:79
  100.6 6.7 %collective-permute-start.24 = (bf16[128,512]{1,0:T(8,128)(2,1)}, bf16[128,512]{1,0:T(8,128)(2,1)S(1)}, u32[]{:S(2)}, u32[]{:S(2)}) collective-permute-start(bf16[128,512]{1,0:T(8,128)(2,1)} %get-tuple-element.35), channel_id=1, source_target_pairs={{0,1},{1,0},{2,3},{3,2},{4,5},{5,4},{6,7},{7,6},{8,9},{9,8},{10,11... | collective-permute-start | bytes 393224 | tf_op jit(solution)/shard_map/ppermute | solution.py:79
  102.5 9.3 %collective-permute-start.25 = (bf16[128,512]{1,0:T(8,128)(2,1)}, bf16[128,512]{1,0:T(8,128)(2,1)S(1)}, u32[]{:S(2)}, u32[]{:S(2)}) collective-permute-start(bf16[128,512]{1,0:T(8,128)(2,1)} %get-tuple-element.36), channel_id=1, source_target_pairs={{0,2},{1,3},{2,0},{3,1},{4,6},{5,7},{6,4},{7,5},{8,10},{9,11},{10,... | collective-permute-start | bytes 393224 | tf_op jit(solution)/shard_map/ppermute | solution.py:79
  104.5 7.2 %collective-permute-start.23 = (bf16[288,128]{1,0:T(8,128)(2,1)S(1)}, bf16[288,128]{1,0:T(8,128)(2,1)S(1)}, u32[]{:S(2)}, u32[]{:S(2)}) collective-permute-start(bf16[288,128]{1,0:T(8,128)(2,1)S(1)} %get-tuple-element.43.refs_0_), channel_id=1, source_target_pairs={{0,24},{8,16},{16,8},{24,0},{1,25},{9,17},{17,9},{25,1},{2,26},{10... | collective-permute-start | bytes 221192 | tf_op jit(solution)/shard_map/ppermute | solution.py:67
  105.8 7.6 %collective-permute-start.22 = (bf16[288,128]{1,0:T(8,128)(2,1)S(1)}, bf16[288,128]{1,0:T(8,128)(2,1)S(1)}, u32[]{:S(2)}, u32[]{:S(2)}) collective-permute-start(bf16[288,128]{1,0:T(8,128)(2,1)S(1)} %get-tuple-element.43.refs_0_), channel_id=1, source_target_pairs={{0,16},{8,24},{16,0},{24,8},{1,17},{9,25},{17,1},{25,9},{2,18},{10... | collective-permute-start | bytes 221192 | tf_op jit(solution)/shard_map/ppermute | solution.py:67
  106.7 8.1 %collective-permute-start.21 = (bf16[288,128]{1,0:T(8,128)(2,1)S(1)}, bf16[288,128]{1,0:T(8,128)(2,1)S(1)}, u32[]{:S(2)}, u32[]{:S(2)}) collective-permute-start(bf16[288,128]{1,0:T(8,128)(2,1)S(1)} %get-tuple-element.43.refs_0_), channel_id=1, source_target_pairs={{0,8},{8,0},{16,24},{24,16},{1,9},{9,1},{17,25},{25,17},{2,10},{10... | collective-permute-start | bytes 221192 | tf_op jit(solution)/shard_map/ppermute | solution.py:67
  107.3 13.3 %collective-permute-start.26 = (bf16[128,512]{1,0:T(8,128)(2,1)S(1)}, bf16[128,512]{1,0:T(8,128)(2,1)S(1)}, u32[]{:S(2)}, u32[]{:S(2)}) collective-permute-start(bf16[128,512]{1,0:T(8,128)(2,1)S(1)} %copy-done.19), channel_id=1, source_target_pairs={{0,3},{1,2},{2,1},{3,0},{4,7},{5,6},{6,5},{7,4},{8,11},{9,10},{10,... | collective-permute-start | bytes 393224 | tf_op jit(solution)/shard_map/ppermute | solution.py:79
  111.7 8.8 %collective-permute-start.27 = (bf16[128,512]{1,0:T(8,128)(2,1)S(1)}, bf16[128,512]{1,0:T(8,128)(2,1)S(1)}, u32[]{:S(2)}, u32[]{:S(2)}) collective-permute-start(bf16[128,512]{1,0:T(8,128)(2,1)S(1)} %copy-done.18), channel_id=1, source_target_pairs={{0,4},{1,5},{2,6},{3,7},{4,0},{5,1},{6,2},{7,3},{8,12},{9,13},{10,... | collective-permute-start | bytes 393224 | tf_op jit(solution)/shard_map/ppermute | solution.py:79
  111.8 16.9 %collective-permute-start.28 = (bf16[128,512]{1,0:T(8,128)(2,1)S(1)}, bf16[128,512]{1,0:T(8,128)(2,1)S(1)}, u32[]{:S(2)}, u32[]{:S(2)}) collective-permute-start(bf16[128,512]{1,0:T(8,128)(2,1)S(1)} %copy-done.17), channel_id=1, source_target_pairs={{0,5},{1,4},{2,7},{3,6},{4,1},{5,0},{6,3},{7,2},{8,13},{9,12},{10,... | collective-permute-start | bytes 393224 | tf_op jit(solution)/shard_map/ppermute | solution.py:79
  113.4 19.4 %collective-permute-start.29 = (bf16[128,512]{1,0:T(8,128)(2,1)S(1)}, bf16[128,512]{1,0:T(8,128)(2,1)S(1)}, u32[]{:S(2)}, u32[]{:S(2)}) collective-permute-start(bf16[128,512]{1,0:T(8,128)(2,1)S(1)} %copy-done.16), channel_id=1, source_target_pairs={{0,6},{1,7},{2,4},{3,5},{4,2},{5,3},{6,0},{7,1},{8,14},{9,15},{10,... | collective-permute-start | bytes 393224 | tf_op jit(solution)/shard_map/ppermute | solution.py:79
  114.7 21.4 %collective-permute-start.30 = (bf16[128,512]{1,0:T(8,128)(2,1)S(1)}, bf16[128,512]{1,0:T(8,128)(2,1)S(1)}, u32[]{:S(2)}, u32[]{:S(2)}) collective-permute-start(bf16[128,512]{1,0:T(8,128)(2,1)S(1)} %copy-done.15), channel_id=1, source_target_pairs={{0,7},{1,6},{2,5},{3,4},{4,3},{5,2},{6,1},{7,0},{8,15},{9,14},{10,... | collective-permute-start | bytes 393224 | tf_op jit(solution)/shard_map/ppermute | solution.py:79
  (29 other events, 551.3 us)
